TPU v7x, 512 devices: a whole 4x8x8 slice. The times are simulated.
512 devices in a mesh: tm: 16 (over z_lo, x, core), height: 32 (over y, z_hi).
Axes of the slice: x: 4, y: 8, z: 8 (z_hi: 4, z_lo: 2; z = z_hi * 2 + z_lo), core: 2. Of those that a mesh axis runs over, the one named last changes fastest.
Arguments:
- video_q: bfloat16 [16, 32, 768, 256], P('tm', 'height'), may hold values from -4.5 to 4.5
- video_k: bfloat16 [16, 32, 768, 256], P('tm', 'height'), may hold values from -4.5 to 4.5
- video_v: bfloat16 [16, 32, 768, 256], P('tm', 'height'), may hold values from -6 to 6
- text_k: bfloat16 [256, 256], P('height'), may hold values from -4.5 to 4.5
- text_v: bfloat16 [256, 256], P('height'), may hold values from -6 to 6
- text_valid: int32 [256], replicated, may hold values from 0 to 1, as said below
- extent: int32 [2, 3], replicated, may hold values from 0 to 1
Outputs:
- video_out: bfloat16 [16, 32, 768, 256], P('tm', 'height')
Inputs may be any that keep to these rules, and one draw needn't show every extreme that they name: `text_valid`: the valid text tokens come first; at least 64 are valid and at least one is not.
All inputs are finite; a program needn't handle non-finite values.
Results may differ from a plain program's by a relative error of at most 0.0042.
Values may be sent and summed in bfloat16 or wider, within the bound.
No kernel may reach another device: no remote copies, remote signals or barrier semaphores. Data moves between devices by JAX's collectives and lax.ppermute only.
A program may use at most 64 MiB of HBM per device.

v0:
```python
import math
import jax
import jax.numpy as jnp
from jax import lax
from jax.sharding import PartitionSpec as P

TILE = 384


def padded_2(array, sides, width):
    for axis, dim in sides:
        size, length = (lax.axis_size(axis), array.shape[dim])
        up = [(i, (i + 1) % size) for i in range(size - 1)]
        down = [(j, i) for i, j in up]
        last = lax.slice_in_dim(array, length - width, length, axis=dim)
        initial = lax.slice_in_dim(array, 0, width, axis=dim)
        before = lax.ppermute(last, axis, up)
        after = lax.ppermute(initial, axis, down)
        array = jnp.concatenate([before, array, after], axis=dim)
    return array


def shards(video_q, video_k, video_v, text_k, text_v, text_valid, extent):
    row_count = video_q.shape[2]
    feat_count = video_q.shape[3]
    head_count = extent.shape[0]
    head_width = feat_count // head_count
    tile_count = row_count // TILE
    score_scale = 1.0 / math.sqrt(head_width)
    key_value = jnp.concatenate((video_k, video_v), axis=3)
    padded = padded_2(key_value, (("tm", 0), ("height", 1)), 1)
    slab_all = padded.reshape(9 * row_count, 2 * feat_count)
    text_keys, text_values = (
        lax.all_gather(text_k, "height", axis=0, tiled=True),
        lax.all_gather(text_v, "height", axis=0, tiled=True),
    )
    time_count = lax.axis_size("tm")
    height_count = lax.axis_size("height")
    local_time = lax.axis_index("tm")
    local_height = lax.axis_index("height")
    key_ids = jnp.arange(9 * row_count, dtype=jnp.int32)
    slab_index = key_ids // row_count
    time_gap = slab_index // 3 - 1
    height_gap = slab_index % 3 - 1
    key_tile = key_ids % row_count // TILE
    inside_keys = (local_time + time_gap >= 0) & (local_time + time_gap < time_count)
    inside_keys = (
        inside_keys & (local_height + height_gap >= 0) & (local_height + height_gap < height_count)
    )
    text_ok = text_valid > 0
    queries = video_q[0, 0].reshape(tile_count, TILE, feat_count)

    def one_block(operands):
        query_block, query_tile = operands
        width_gap = jnp.abs(key_tile - query_tile)
        head_outputs = []
        for head_index in range(head_count):
            low = head_index * head_width
            high = low + head_width
            allowed = (
                inside_keys
                & (jnp.abs(time_gap) <= extent[head_index, 0])
                & (jnp.abs(height_gap) <= extent[head_index, 1])
            )
            allowed = allowed & (width_gap <= extent[head_index, 2])
            query_head = query_block[:, low:high]
            video_scores = (
                jnp.einsum(
                    "qd,kd->qk",
                    query_head,
                    slab_all[:, low:high],
                    preferred_element_type=jnp.float32,
                )
                * score_scale
            )
            text_scores = (
                jnp.einsum(
                    "qd,kd->qk",
                    query_head,
                    text_keys[:, low:high],
                    preferred_element_type=jnp.float32,
                )
                * score_scale
            )
            video_scores = jnp.where(allowed[None, :], video_scores, -jnp.inf)
            text_scores = jnp.where(text_ok[None, :], text_scores, -jnp.inf)
            row_top = jnp.maximum(jnp.max(video_scores, axis=1), jnp.max(text_scores, axis=1))
            video_expo = jnp.exp(video_scores - row_top[:, None])
            text_expo = jnp.exp(text_scores - row_top[:, None])
            row_total = jnp.sum(video_expo, axis=1) + jnp.sum(text_expo, axis=1)
            value_low = feat_count + low
            weighted = jnp.dot(
                video_expo.astype(jnp.bfloat16),
                slab_all[:, value_low : value_low + head_width],
                preferred_element_type=jnp.float32,
            )
            weighted = weighted + jnp.dot(
                text_expo.astype(jnp.bfloat16),
                text_values[:, low:high],
                preferred_element_type=jnp.float32,
            )
            head_outputs.append(weighted / row_total[:, None])
        return jnp.concatenate(head_outputs, axis=1).astype(jnp.bfloat16)

    blocks = lax.map(one_block, (queries, jnp.arange(tile_count, dtype=jnp.int32)))
    return blocks.reshape(video_q.shape)


def solution(mesh):
    return jax.shard_map(
        shards,
        mesh=mesh,
        in_specs=(
            P("tm", "height", None, None),
            P("tm", "height", None, None),
            P("tm", "height", None, None),
            P("height", None),
            P("height", None),
            P(),
            P(),
        ),
        out_specs=P("tm", "height", None, None),
        check_vma=False,
    )
```

profile of v0, /device:TPU:4, one launch (start us, length us, event | category | flops | bytes accessed | tf_op | source)
XLA Modules:
  0.0 332.3 jit_solution(4440091307780463444)
XLA Ops:
  0.0 1.0 constant_dynamic-update-slice_fusion.2
  1.0 1.0 constant_dynamic-update-slice_fusion.1
  2.1 1.9 collective-permute-start
  4.0 3.6 %collective-permute-start.1 = (bf16[1,1,768,512]{3,2,1,0:T(8,128)(2,1)S(1)}, bf16[1,1,768,512]{3,2,1,0:T(8,128)(2,1)S(1)}, u32[]{:S(2)}, u32[]{:S(2)}) collective-permute-start(bf16[1,1,768,512]{3,2,1,0:T(8,128)(2,1)S(1)} %constant_dynamic-update-slice_fusion.1), channel_id=1, source_target_pairs={{32,0},{64,32},{96,64},{128,96},{160,128},{192,160},{224,192},{256... | collective-permute-start | bytes 2359304 | tf_op jit(solution)/shard_map/ppermute | solution.py:18
  7.6 7.7 %collective-permute-done = bf16[1,1,768,512]{3,2,1,0:T(8,128)(2,1)S(1)} collective-permute-done((bf16[1,1,768,512]{3,2,1,0:T(8,128)(2,1)S(1)}, bf16[1,1,768,512]{3,2,1,0:T(8,128)(2,1)S(1)}, u32[]{:S(2)}, u32[]{:S(2)}) %collective-permute-start) | collective-permute-done | bytes 786464 | tf_op jit(solution)/shard_map/ppermute | solution.py:17
  15.4 1.8 collective-permute-done.1
  17.1 1.7 pad_maximum_fusion.2
  18.8 7.5 %collective-permute-start.2 = (bf16[3,1,768,512]{3,2,1,0:T(8,128)(2,1)}, bf16[3,1,768,512]{3,2,1,0:T(8,128)(2,1)}, u32[]{:S(2)}, u32[]{:S(2)}) collective-permute-start(bf16[3,1,768,512]{3,2,1,0:T(8,128)(2,1)} %pad_maximum_fusion.2), channel_id=1, source_target_pairs={{0,1},{1,2},{2,3},{3,4},{4,5},{5,6},{6,7},{7,8},{8,9},{9,10},{10,1... | collective-permute-start | bytes 7077896 | tf_op jit(solution)/shard_map/ppermute | solution.py:17
  26.3 1.3 collective-permute-start.3
  27.6 179.9 %all_gather.6 = bf16[256,256]{1,0:T(8,128)(2,1)S(1)} all-gather(bf16[8,256]{1,0:T(8,128)(2,1)} %param.12), channel_id=1, replica_groups=mesh['tm'=16,'height'=32] {'height'}, dimensions={0}, use_global_device_ids=true | all-gather | bytes 135168 | tf_op jit(solution)/shard_map/all_gather | solution.py:34
  207.5 76.3 %all_gather.7 = bf16[256,256]{1,0:T(8,128)(2,1)S(1)} all-gather(bf16[8,256]{1,0:T(8,128)(2,1)} %param.13), channel_id=1, replica_groups=mesh['tm'=16,'height'=32] {'height'}, dimensions={0}, use_global_device_ids=true | all-gather | bytes 135168 | tf_op jit(solution)/shard_map/all_gather | solution.py:35
  284.4 5.9 %pad_maximum_fusion.1 = bf16[3,3,768,512]{3,2,1,0:T(8,128)(2,1)} fusion(bf16[3,1,768,512]{3,2,1,0:T(8,128)(2,1)} %collective-permute-done.3, bf16[1,1,768,512]{3,2,1,0:T(8,128)(2,1)S(1)} %collective-permute-done.1, bf16[1,1,768,512]{3,2,1,0:T(8,128)(2,1)S(1)} %constant_dynamic-update-slice_fusion.1, bf16[1,1,768,512]{3,2,1,0:T(8,128)(2,1)S(1)} %collective-permute-done, ...), kind=kLoop, calls=%fused_computation.95 | loop fusion | flops 14155776 | bytes 14155776 | tf_op jit(solution)/shard_map/concatenate | solution.py:19
  290.3 41.2 %while.15 = (s32[]{:T(128)}, bf16[2,384,256]{2,1,0:T(8,128)(2,1)S(1)}, s32[2,3]{1,0:T(2,128)S(1)}, s32[2]{0:T(128)S(1)}, bf16[2,384,256]{2,1,0:T(8,128)(2,1)S(1)...) while((s32[]{:T(128)}, ...), condition=%wide.region_9.10_spmd.clone.clone, body=%wide.region_0.9_spmd.clone.clone.sunk | while | flops 2858657792 | bytes 97717000 | solution.py:105
  291.0 0.9 compare_reduce_fusion.10
  292.0 1.0 compare_reduce_fusion.11
  293.8 1.0 compare_reduce_fusion.9
  295.3 1.9 compare_and_fusion.4
  297.3 3.3 fusion.109
  300.8 1.6 fusion.112
  302.6 2.0 fusion.111
  304.8 1.7 fusion.103
  306.9 1.6 fusion.106
  308.5 2.0 fusion.105
  312.6 1.0 compare_reduce_fusion.11
  314.4 1.0 compare_reduce_fusion.9
  316.0 1.9 compare_and_fusion.4
  317.9 3.3 fusion.109
  321.5 1.6 fusion.112
  323.2 2.0 fusion.111
  325.5 1.7 fusion.103
  327.5 1.6 fusion.106
  329.1 2.0 fusion.105
  (56 shorter events, 9.4 us)
Async XLA Ops:
  2.1 13.3 %collective-permute-start = (bf16[1,1,768,512]{3,2,1,0:T(8,128)(2,1)S(1)}, bf16[1,1,768,512]{3,2,1,0:T(8,128)(2,1)S(1)}, u32[]{:S(2)}, u32[]{:S(2)}) collective-permute-start(bf16[1,1,768,512]{3,2,1,0:T(8,128)(2,1)S(1)} %constant_dynamic-update-slice_fusion.1), channel_id=1, source_target_pairs={{0,32},{32,64},{64,96},{96,128},{128,160},{160,192},{192,224},{224... | collective-permute-start | bytes 2359304 | tf_op jit(solution)/shard_map/ppermute | solution.py:17
  4.0 13.1 %collective-permute-start.1 = (bf16[1,1,768,512]{3,2,1,0:T(8,128)(2,1)S(1)}, bf16[1,1,768,512]{3,2,1,0:T(8,128)(2,1)S(1)}, u32[]{:S(2)}, u32[]{:S(2)}) collective-permute-start(bf16[1,1,768,512]{3,2,1,0:T(8,128)(2,1)S(1)} %constant_dynamic-update-slice_fusion.1), channel_id=1, source_target_pairs={{32,0},{64,32},{96,64},{128,96},{160,128},{192,160},{224,192},{256... | collective-permute-start | bytes 2359304 | tf_op jit(solution)/shard_map/ppermute | solution.py:18
  18.8 265.6 %collective-permute-start.2 = (bf16[3,1,768,512]{3,2,1,0:T(8,128)(2,1)}, bf16[3,1,768,512]{3,2,1,0:T(8,128)(2,1)}, u32[]{:S(2)}, u32[]{:S(2)}) collective-permute-start(bf16[3,1,768,512]{3,2,1,0:T(8,128)(2,1)} %pad_maximum_fusion.2), channel_id=1, source_target_pairs={{0,1},{1,2},{2,3},{3,4},{4,5},{5,6},{6,7},{7,8},{8,9},{9,10},{10,1... | collective-permute-start | bytes 7077896 | tf_op jit(solution)/shard_map/ppermute | solution.py:17
  26.3 258.2 %collective-permute-start.3 = (bf16[3,1,768,512]{3,2,1,0:T(8,128)(2,1)}, bf16[3,1,768,512]{3,2,1,0:T(8,128)(2,1)}, u32[]{:S(2)}, u32[]{:S(2)}) collective-permute-start(bf16[3,1,768,512]{3,2,1,0:T(8,128)(2,1)} %pad_maximum_fusion.2), channel_id=1, source_target_pairs={{1,0},{2,1},{3,2},{4,3},{5,4},{6,5},{7,6},{8,7},{9,8},{10,9},{11,1... | collective-permute-start | bytes 7077896 | tf_op jit(solution)/shard_map/ppermute | solution.py:18
  284.4 5.9 %copy-start = (bf16[1,1,768,256]{3,2,1,0:T(8,128)(2,1)S(1)}, bf16[1,1,768,256]{3,2,1,0:T(8,128)(2,1)}, u32[]{:S(2)}) copy-start(bf16[1,1,768,256]{3,2,1,0:T(8,128)(2,1)} %param.9) | copy-start | bytes 1179652
  284.4 5.9 %copy-start.1 = (s32[2,3]{1,0:T(2,128)S(1)}, s32[2,3]{1,0:T(2,128)}, u32[]{:S(2)}) copy-start(s32[2,3]{1,0:T(2,128)} %param.15) | copy-start | bytes 76
  297.3 5.3 %slice-start = ((s8[7077888]{0:T(1024)(128)(4,1)}), s8[4194304]{0:T(1024)(128)(4,1)S(1)}, s32[]{:S(2)}) async-start(s8[7077888]{0:T(1024)(128)(4,1)} %bitcast.37), calls=%async_computation | async-start | bytes 8388608 | tf_op jit(solution)/shard_map/while
  297.3 5.3 %slice-start.1 = ((s8[7077888]{0:T(1024)(128)(4,1)}), s8[2883584]{0:T(1024)(128)(4,1)S(1)}, s32[]{:S(2)}) async-start(s8[7077888]{0:T(1024)(128)(4,1)} %bitcast.37), calls=%async_computation.1 | async-start | bytes 5767168 | tf_op jit(solution)/shard_map/while
  317.9 5.3 %slice-start = ((s8[7077888]{0:T(1024)(128)(4,1)}), s8[4194304]{0:T(1024)(128)(4,1)S(1)}, s32[]{:S(2)}) async-start(s8[7077888]{0:T(1024)(128)(4,1)} %bitcast.37), calls=%async_computation | async-start | bytes 8388608 | tf_op jit(solution)/shard_map/while
  317.9 5.3 %slice-start.1 = ((s8[7077888]{0:T(1024)(128)(4,1)}), s8[2883584]{0:T(1024)(128)(4,1)S(1)}, s32[]{:S(2)}) async-start(s8[7077888]{0:T(1024)(128)(4,1)} %bitcast.37), calls=%async_computation.1 | async-start | bytes 5767168 | tf_op jit(solution)/shard_map/while
  331.6 0.7 copy-start.2
where the time goes:
time: 333 us; the launch traced here: 332 us
  blocking collectives  256 us (77%)
  other arithmetic  26.5 us (8%)
  matrix products  19.8 us (6%)
  starting transfers between devices  14.3 us (4%)
  waiting for transfers between devices  9.49 us (3%)
  local copies, waits for them, and re-layouts  5.73 us (2%)
    all_gather x1, blocking collectives, shards(): lax.all_gather(text_k, 'height', axis=0, tiled=True)  180 us
    all_gather x1, blocking collectives, shards(): lax.all_gather(text_v, 'height', axis=0, tiled=True)  76.3 us
    dot_general x4, matrix products, one_block(): jnp.einsum('qd,kd->qk', query_head, slab_all[:, low:high], preferred_elem...  9.85 us
    ppermute x2, starting transfers between devices, padded_2(): before = lax.ppermute(last, axis, up)  9.4 us
    dot_general x4, matrix products, one_block(): jnp.dot(video_expo.astype(jnp.bfloat16), slab_all[:, value_low:value_low...  7.99 us
    ppermute x2, waiting for transfers between devices, padded_2(): before = lax.ppermute(last, axis, up)  7.73 us
    concatenate x2, other arithmetic, padded_2(): array = jnp.concatenate([before, array, after], axis=dim)  7.55 us
    reduce_sum x8, other arithmetic, one_block(): row_total = jnp.sum(video_expo, axis=1) + jnp.sum(text_expo, axis=1)  6.88 us
  transfers between devices with their start and end apart: 4, of which 2 were waited for; matrix products, arithmetic and copies ran while one was open for 0% of the time, Pallas kernels for 0%

commit v1 on v0

--- a/solution.py
+++ b/solution.py
@@ -31,7 +31,9 @@
     padded = padded_2(key_value, (("tm", 0), ("height", 1)), 1)
     slab_all = padded.reshape(9 * row_count, 2 * feat_count)
     text_keys, text_values = (
-        lax.all_gather(text_k, "height", axis=0, tiled=True),
+        jnp.concatenate(
+            lax.all_to_all(jnp.stack([text_k] * lax.axis_size("height")), "height", 0, 0), axis=0
+        ),
         lax.all_gather(text_v, "height", axis=0, tiled=True),
     )
     time_count = lax.axis_size("tm")

time: 333 us -> 261 us (0.78)
  the two profiles are of different devices: /device:TPU:4 before, /device:TPU:68 now
where the time goes in v1:
time: 261 us
  blocking collectives  169 us (65%)
  starting transfers between devices  28.5 us (11%)
  other arithmetic  26.5 us (10%)
  matrix products  19.8 us (8%)
  waiting for transfers between devices  9.49 us (4%)
  local copies, waits for them, and re-layouts  7.14 us (3%)
    all_gather x1, blocking collectives, shards(): lax.all_gather(text_v, 'height', axis=0, tiled=True)  169 us
    all_to_all x1, starting transfers between devices, shards(): lax.all_to_all(jnp.stack([text_k] * lax.axis_size('height')), 'height', 0...  14.2 us
    dot_general x4, matrix products, one_block(): jnp.einsum('qd,kd->qk', query_head, slab_all[:, low:high], preferred_elem...  9.85 us
    ppermute x2, starting transfers between devices, padded_2(): before = lax.ppermute(last, axis, up)  9.4 us
    dot_general x4, matrix products, one_block(): jnp.dot(video_expo.astype(jnp.bfloat16), slab_all[:, value_low:value_low...  7.99 us
    ppermute x2, waiting for transfers between devices, padded_2(): before = lax.ppermute(last, axis, up)  7.73 us
    concatenate x2, other arithmetic, padded_2(): array = jnp.concatenate([before, array, after], axis=dim)  7.55 us
    reduce_sum x8, other arithmetic, one_block(): row_total = jnp.sum(video_expo, axis=1) + jnp.sum(text_expo, axis=1)  6.88 us
  transfers between devices with their start and end apart: 5, of which 2 were waited for; matrix products, arithmetic and copies ran while one was open for 3% of the time, Pallas kernels for 0%

profile of v1, /device:TPU:68, one launch (start us, length us, event | category | flops | bytes accessed | tf_op | source)
XLA Modules:
  0.0 260.6 jit_solution(3654370352824856805)
XLA Ops:
  0.0 1.0 constant_dynamic-update-slice_fusion.2
  1.0 1.0 constant_dynamic-update-slice_fusion.1
  2.1 1.9 collective-permute-start
  4.0 3.6 %collective-permute-start.1 = (bf16[1,1,768,512]{3,2,1,0:T(8,128)(2,1)S(1)}, bf16[1,1,768,512]{3,2,1,0:T(8,128)(2,1)S(1)}, u32[]{:S(2)}, u32[]{:S(2)}) collective-permute-start(bf16[1,1,768,512]{3,2,1,0:T(8,128)(2,1)S(1)} %constant_dynamic-update-slice_fusion.1), channel_id=1, source_target_pairs={{32,0},{64,32},{96,64},{128,96},{160,128},{192,160},{224,192},{256... | collective-permute-start | bytes 2359304 | tf_op jit(solution)/shard_map/ppermute | solution.py:18
  7.6 7.7 %collective-permute-done = bf16[1,1,768,512]{3,2,1,0:T(8,128)(2,1)S(1)} collective-permute-done((bf16[1,1,768,512]{3,2,1,0:T(8,128)(2,1)S(1)}, bf16[1,1,768,512]{3,2,1,0:T(8,128)(2,1)S(1)}, u32[]{:S(2)}, u32[]{:S(2)}) %collective-permute-start) | collective-permute-done | bytes 786464 | tf_op jit(solution)/shard_map/ppermute | solution.py:17
  15.4 1.8 collective-permute-done.1
  17.1 1.7 pad_maximum_fusion.2
  18.8 7.5 %collective-permute-start.2 = (bf16[3,1,768,512]{3,2,1,0:T(8,128)(2,1)}, bf16[3,1,768,512]{3,2,1,0:T(8,128)(2,1)}, u32[]{:S(2)}, u32[]{:S(2)}) collective-permute-start(bf16[3,1,768,512]{3,2,1,0:T(8,128)(2,1)} %pad_maximum_fusion.2), channel_id=1, source_target_pairs={{0,1},{1,2},{2,3},{3,4},{4,5},{5,6},{6,7},{7,8},{8,9},{9,10},{10,1... | collective-permute-start | bytes 7077896 | tf_op jit(solution)/shard_map/ppermute | solution.py:17
  26.3 1.3 collective-permute-start.3
  27.6 1.4 stack.2
  28.9 14.2 %all-to-all-start = ((bf16[32,8,256]{2,1,0:T(8,128)(2,1)}), bf16[32,8,256]{2,1,0:T(8,128)(2,1)S(1)}, u32[]{:S(2)}, u32[]{:S(2)}) async-start(bf16[32,8,256]{2,1,0:T(8,128)(2,1)} %stack.2), calls=%async_computation | async-start | bytes 262144 | tf_op jit(solution)/shard_map/all_to_all | solution.py:35
  43.2 168.8 %all_gather.3 = bf16[256,256]{1,0:T(8,128)(2,1)S(1)} all-gather(bf16[8,256]{1,0:T(8,128)(2,1)} %param.13), channel_id=1, replica_groups=mesh['tm'=16,'height'=32] {'height'}, dimensions={0}, use_global_device_ids=true | all-gather | bytes 135168 | tf_op jit(solution)/shard_map/all_gather | solution.py:37
  212.6 5.9 %pad_maximum_fusion.1 = bf16[3,3,768,512]{3,2,1,0:T(8,128)(2,1)} fusion(bf16[3,1,768,512]{3,2,1,0:T(8,128)(2,1)} %collective-permute-done.3, bf16[1,1,768,512]{3,2,1,0:T(8,128)(2,1)S(1)} %collective-permute-done.1, bf16[1,1,768,512]{3,2,1,0:T(8,128)(2,1)S(1)} %constant_dynamic-update-slice_fusion.1, bf16[1,1,768,512]{3,2,1,0:T(8,128)(2,1)S(1)} %collective-permute-done, ...), kind=kLoop, calls=%fused_computation.95 | loop fusion | flops 14155776 | bytes 14155776 | tf_op jit(solution)/shard_map/concatenate | solution.py:19
  218.5 41.3 %while.15 = (s32[]{:T(128)}, bf16[2,384,256]{2,1,0:T(8,128)(2,1)S(1)}, s32[2,3]{1,0:T(2,128)S(1)}, s32[2]{0:T(128)S(1)}, bf16[2,384,256]{2,1,0:T(8,128)(2,1)S(1)...) while((s32[]{:T(128)}, ...), condition=%wide.region_9.10_spmd.clone.clone, body=%wide.region_0.9_spmd.clone.clone.sunk | while | flops 2858657792 | bytes 97717000 | solution.py:107
  219.2 0.9 compare_reduce_fusion.10
  220.2 1.0 compare_reduce_fusion.11
  223.5 2.0 compare_and_fusion.4
  225.5 3.3 %fusion.109 = (f32[384]{0:T(512)S(1)}, f32[384,6912]{1,0:T(8,128)S(1)}) fusion(bf16[6912,512]{1,0:T(8,128)(2,1)} %get-tuple-element.428, bf16[384,256]{1,0:T(8,128)(2,1)S(1)} %dynamic-slice_bitcast_fusion.2, pred[6912]{0:T(1024)(128)(4,1)S(1)} %get-tuple-element.394), kind=kOutput, calls=%fused_computation.103.clone.1 | convolution fusion | flops 687439488 | bytes 12493312 | tf_op jit(solution)/shard_map/while/body/eval_jaxpr/qd,kd->qk/dot_general | solution.py:70
  229.1 1.6 fusion.112
  230.8 2.0 fusion.111
  233.1 1.7 fusion.103
  235.1 1.6 fusion.106
  236.7 2.0 fusion.105
  239.9 0.9 compare_reduce_fusion.10
  240.8 1.0 compare_reduce_fusion.11
  244.1 2.0 compare_and_fusion.4
  246.2 3.3 %fusion.109 = (f32[384]{0:T(512)S(1)}, f32[384,6912]{1,0:T(8,128)S(1)}) fusion(bf16[6912,512]{1,0:T(8,128)(2,1)} %get-tuple-element.428, bf16[384,256]{1,0:T(8,128)(2,1)S(1)} %dynamic-slice_bitcast_fusion.2, pred[6912]{0:T(1024)(128)(4,1)S(1)} %get-tuple-element.394), kind=kOutput, calls=%fused_computation.103.clone.1 | convolution fusion | flops 687439488 | bytes 12493312 | tf_op jit(solution)/shard_map/while/body/eval_jaxpr/qd,kd->qk/dot_general | solution.py:70
  249.7 1.6 fusion.112
  251.5 2.0 fusion.111
  253.7 1.7 fusion.103
  255.7 1.6 fusion.106
  257.4 2.0 fusion.105
  (58 shorter events, 10.3 us)
Async XLA Ops:
  2.1 13.3 %collective-permute-start = (bf16[1,1,768,512]{3,2,1,0:T(8,128)(2,1)S(1)}, bf16[1,1,768,512]{3,2,1,0:T(8,128)(2,1)S(1)}, u32[]{:S(2)}, u32[]{:S(2)}) collective-permute-start(bf16[1,1,768,512]{3,2,1,0:T(8,128)(2,1)S(1)} %constant_dynamic-update-slice_fusion.1), channel_id=1, source_target_pairs={{0,32},{32,64},{64,96},{96,128},{128,160},{160,192},{192,224},{224... | collective-permute-start | bytes 2359304 | tf_op jit(solution)/shard_map/ppermute | solution.py:17
  4.0 13.1 %collective-permute-start.1 = (bf16[1,1,768,512]{3,2,1,0:T(8,128)(2,1)S(1)}, bf16[1,1,768,512]{3,2,1,0:T(8,128)(2,1)S(1)}, u32[]{:S(2)}, u32[]{:S(2)}) collective-permute-start(bf16[1,1,768,512]{3,2,1,0:T(8,128)(2,1)S(1)} %constant_dynamic-update-slice_fusion.1), channel_id=1, source_target_pairs={{32,0},{64,32},{96,64},{128,96},{160,128},{192,160},{224,192},{256... | collective-permute-start | bytes 2359304 | tf_op jit(solution)/shard_map/ppermute | solution.py:18
  18.8 193.8 %collective-permute-start.2 = (bf16[3,1,768,512]{3,2,1,0:T(8,128)(2,1)}, bf16[3,1,768,512]{3,2,1,0:T(8,128)(2,1)}, u32[]{:S(2)}, u32[]{:S(2)}) collective-permute-start(bf16[3,1,768,512]{3,2,1,0:T(8,128)(2,1)} %pad_maximum_fusion.2), channel_id=1, source_target_pairs={{0,1},{1,2},{2,3},{3,4},{4,5},{5,6},{6,7},{7,8},{8,9},{9,10},{10,1... | collective-permute-start | bytes 7077896 | tf_op jit(solution)/shard_map/ppermute | solution.py:17
  26.3 186.4 %collective-permute-start.3 = (bf16[3,1,768,512]{3,2,1,0:T(8,128)(2,1)}, bf16[3,1,768,512]{3,2,1,0:T(8,128)(2,1)}, u32[]{:S(2)}, u32[]{:S(2)}) collective-permute-start(bf16[3,1,768,512]{3,2,1,0:T(8,128)(2,1)} %pad_maximum_fusion.2), channel_id=1, source_target_pairs={{1,0},{2,1},{3,2},{4,3},{5,4},{6,5},{7,6},{8,7},{9,8},{10,9},{11,1... | collective-permute-start | bytes 7077896 | tf_op jit(solution)/shard_map/ppermute | solution.py:18
  28.9 189.6 %all-to-all-start = ((bf16[32,8,256]{2,1,0:T(8,128)(2,1)}), bf16[32,8,256]{2,1,0:T(8,128)(2,1)S(1)}, u32[]{:S(2)}, u32[]{:S(2)}) async-start(bf16[32,8,256]{2,1,0:T(8,128)(2,1)} %stack.2), calls=%async_computation | async-start | bytes 262144 | tf_op jit(solution)/shard_map/all_to_all | solution.py:35
  212.6 5.9 %copy-start = (bf16[1,1,768,256]{3,2,1,0:T(8,128)(2,1)S(1)}, bf16[1,1,768,256]{3,2,1,0:T(8,128)(2,1)}, u32[]{:S(2)}) copy-start(bf16[1,1,768,256]{3,2,1,0:T(8,128)(2,1)} %param.9) | copy-start | bytes 1179652
  212.6 5.9 %copy-start.1 = (s32[2,3]{1,0:T(2,128)S(1)}, s32[2,3]{1,0:T(2,128)}, u32[]{:S(2)}) copy-start(s32[2,3]{1,0:T(2,128)} %param.15) | copy-start | bytes 76
  225.5 5.3 %slice-start = ((s8[7077888]{0:T(1024)(128)(4,1)}), s8[4194304]{0:T(1024)(128)(4,1)S(1)}, s32[]{:S(2)}) async-start(s8[7077888]{0:T(1024)(128)(4,1)} %bitcast.38), calls=%async_computation.1 | async-start | bytes 8388608 | tf_op jit(solution)/shard_map/while
  225.5 5.3 %slice-start.1 = ((s8[7077888]{0:T(1024)(128)(4,1)}), s8[2883584]{0:T(1024)(128)(4,1)S(1)}, s32[]{:S(2)}) async-start(s8[7077888]{0:T(1024)(128)(4,1)} %bitcast.38), calls=%async_computation.2 | async-start | bytes 5767168 | tf_op jit(solution)/shard_map/while
  246.2 5.3 %slice-start = ((s8[7077888]{0:T(1024)(128)(4,1)}), s8[4194304]{0:T(1024)(128)(4,1)S(1)}, s32[]{:S(2)}) async-start(s8[7077888]{0:T(1024)(128)(4,1)} %bitcast.38), calls=%async_computation.1 | async-start | bytes 8388608 | tf_op jit(solution)/shard_map/while
  246.2 5.3 %slice-start.1 = ((s8[7077888]{0:T(1024)(128)(4,1)}), s8[2883584]{0:T(1024)(128)(4,1)S(1)}, s32[]{:S(2)}) async-start(s8[7077888]{0:T(1024)(128)(4,1)} %bitcast.38), calls=%async_computation.2 | async-start | bytes 5767168 | tf_op jit(solution)/shard_map/while
  259.8 0.7 copy-start.2
